TPU v7x, 32 devices: a whole 2x2x4 slice. The times are simulated.
32 devices in a mesh: row: 4 (over y, x), col: 8 (over z, core).
Axes of the slice: x: 2, y: 2, z: 4, core: 2. Of those that a mesh axis runs over, the one named last changes fastest.
Arguments:
- integrals: bfloat16 [800, 800, 640], P('row', 'col'), may hold values from -0.625 to 0.625
- amplitudes: bfloat16 [1024, 640], P('row', 'col'), may hold values from -6 to 6
- virt_irrep: int32 [800], replicated, may hold values from 0 to 7, as said below
- pair_irrep: int32 [640], replicated, may hold values from 0 to 7, as said below
- virt_energy: float32 [800], replicated, may hold values from 0.3 to 4
- occ_energy: float32 [32], replicated, may hold values from -2 to -0.3
Outputs:
- update: bfloat16 [800, 800, 1024], P('row', 'col')
Inputs may be any that keep to these rules, and one draw needn't show every extreme that they name: `virt_irrep`: labels never fall along the index; each of the 8 labels covers one contiguous run of at least 66 orbitals. `pair_irrep`: labels never fall along the index; each of the 8 labels covers one contiguous run of at least 53 pairs.
All inputs are finite; a program needn't handle non-finite values.
Results may differ from a plain program's by a relative error of at most 0.0049.
Values may be sent and summed in bfloat16 or wider, within the bound.
No kernel may reach another device: no remote copies, remote signals or barrier semaphores. Data moves between devices by JAX's collectives and lax.ppermute only.
A program may use at most 320 MiB of HBM per device.

v0:
```python
import jax
import jax.numpy as jnp
from jax import lax
from jax.sharding import PartitionSpec as P


def pair_swapper(occupied):
    pairs = occupied * occupied
    source = jnp.arange(pairs, dtype=jnp.int32)
    target = source % occupied * occupied + source // occupied
    return (source[:, None] == target[None, :]).astype(jnp.bfloat16)


def per_device(integrals, amplitudes, virt_irrep, pair_irrep, virt_energy, occ_energy):
    tile_a, tile_b, slab = integrals.shape
    occupied = occ_energy.shape[0]
    pairs = occupied * occupied
    row_at = lax.axis_index("row")
    col_at = lax.axis_index("col")
    labels_a = lax.dynamic_slice_in_dim(virt_irrep, row_at * tile_a, tile_a, 0)
    labels_b = lax.dynamic_slice_in_dim(virt_irrep, col_at * tile_b, tile_b, 0)
    keep = (
        jnp.bitwise_xor(labels_a[:, None, None], labels_b[None, :, None])
        == pair_irrep[None, None, :]
    )
    masked = jnp.where(keep, integrals, jnp.zeros((), integrals.dtype))
    flat = masked.reshape(tile_a * tile_b, slab)
    swapper = pair_swapper(occupied)
    first_move = lax.all_to_all(masked, "row", split_axis=2, concat_axis=0, tiled=True)
    second_move = lax.all_to_all(first_move, "col", split_axis=0, concat_axis=1, tiled=True)
    third_move = lax.all_to_all(second_move, "row", split_axis=1, concat_axis=2, tiled=True)
    mirrored = jnp.transpose(third_move, (1, 0, 2)).reshape(tile_a * tile_b, slab)
    stacked = jnp.concatenate([flat, mirrored], axis=0)
    all_pairs = lax.all_gather(amplitudes, "row", axis=0, tiled=True)
    totals = lax.dot_general(
        stacked,
        lax.all_gather(all_pairs, "col", axis=1, tiled=True),
        (((1,), (1,)), ((), ())),
        preferred_element_type=jnp.float32,
    )
    rounded = totals.astype(jnp.bfloat16)
    ladder = rounded[: tile_a * tile_b].reshape(tile_a, tile_b, pairs)
    swapped = rounded[tile_a * tile_b :]
    other = jnp.dot(swapped, swapper, preferred_element_type=jnp.float32).reshape(
        tile_a, tile_b, pairs
    )
    energy_a = lax.dynamic_slice_in_dim(virt_energy, row_at * tile_a, tile_a, 0)
    energy_b = lax.dynamic_slice_in_dim(virt_energy, col_at * tile_b, tile_b, 0)
    pair_energy = (occ_energy[:, None] + occ_energy[None, :]).reshape(pairs)
    denom = energy_a[:, None, None] + energy_b[None, :, None] - pair_energy[None, None, :]
    return ((ladder.astype(jnp.float32) + other) / denom).astype(jnp.bfloat16)


def solution(mesh):
    return jax.shard_map(
        per_device,
        mesh=mesh,
        in_specs=(P("row", "col", None), P("row", "col"), P(), P(), P(), P()),
        out_specs=P("row", "col", None),
        check_vma=False,
    )
```

profile of v0, /device:TPU:0, one launch (start us, length us, event | category | flops | bytes accessed | tf_op | source)
XLA Modules:
  0.0 2155.1 jit_solution(9349818439057503624)
XLA Ops:
  6.5 0.0 copy-start.4
  6.5 0.8 dynamic_slice.12
  7.3 0.8 dynamic_slice.13
  8.1 44.4 %copy.26 = bf16[200,100,640]{1,0,2:T(8,128)(2,1)} copy(bf16[200,100,640]{2,0,1:T(8,128)(2,1)} %param.6) | data formatting | bytes 51200000 | tf_op args[0]
  52.5 0.1 broadcast_xor_fusion
  52.6 0.0 copy-done.4
  52.6 22.7 %compare_select_fusion = bf16[200,100,640]{1,0,2:T(8,128)(2,1)} fusion(bf16[200,100,640]{1,0,2:T(8,128)(2,1)} %copy.26, s32[200,100]{1,0:T(8,128)S(1)} %broadcast_xor_fusion, s32[640]{0:T(1024)S(1)} %copy-done.4), kind=kLoop, calls=%fused_computation.3 | loop fusion | flops 25600000 | bytes 51282560 | tf_op jit(solution)/shard_map/jit(_where)/select_n | solution.py:26
  75.3 373.5 %all_to_all.54 = bf16[200,100,640]{1,0,2:T(8,128)(2,1)} all-to-all(bf16[200,100,640]{1,0,2:T(8,128)(2,1)} %compare_select_fusion), channel_id=1, replica_groups=mesh['row'=4,'col'=8] {'row'}, dimensions={2} | all-to-all | bytes 51200000 | tf_op jit(solution)/shard_map/all_to_all | solution.py:29
  448.8 22.7 %copy.39 = bf16[4,200,100,160]{2,3,1,0:T(8,128)(2,1)} copy(bf16[4,200,100,160]{2,1,3,0:T(8,128)(2,1)} %bitcast.24) | data formatting | bytes 51200000 | tf_op jit(solution)/shard_map/all_to_all | solution.py:29
  471.4 717.3 %all_to_all.55 = bf16[800,100,160]{1,2,0:T(8,128)(2,1)} all-to-all(bf16[800,100,160]{1,2,0:T(8,128)(2,1)} %bitcast.20), channel_id=1, replica_groups=mesh['row'=4,'col'=8] {'col'}, dimensions={0} | all-to-all | bytes 51200000 | tf_op jit(solution)/shard_map/all_to_all | solution.py:30
  1188.7 53.0 %copy.40 = bf16[100,8,100,160]{0,3,2,1:T(8,128)(2,1)} copy(bf16[100,8,100,160]{2,3,0,1:T(8,128)(2,1)} %bitcast.21) | data formatting | bytes 51200000 | tf_op jit(solution)/shard_map/all_to_all | solution.py:30
  1241.7 0.0 copy-start.2
  1241.7 9.7 all-to-all-start.2
  1251.4 0.0 all-gather.2.cloned.1.call-start
  1251.5 0.0 copy-done.2
  1251.5 358.5 %all_gather.6 = bf16[1024,80]{0,1:T(8,128)(2,1)} all-gather(bf16[256,80]{0,1:T(8,128)(2,1)S(1)} %copy-done.2), channel_id=1, replica_groups=mesh['row'=4,'col'=8] {'row'}, dimensions={0}, use_global_device_ids=true | all-gather | bytes 204800 | tf_op jit(solution)/shard_map/all_gather | solution.py:34
  1610.0 0.0 all-gather.2.cloned.1.call-update
  1610.0 0.0 copy-start.5
  1610.0 42.8 %reshape.115 = bf16[20000,640]{0,1:T(8,128)(2,1)} reshape(bf16[200,100,640]{1,0,2:T(8,128)(2,1)} %compare_select_fusion) | data formatting | bytes 51200000 | tf_op jit(solution)/shard_map/reshape | solution.py:27
  1652.8 0.8 dynamic_slice.14
  1653.6 0.8 dynamic_slice.15
  1654.3 31.7 %copy.37 = bf16[20000,640]{1,0:T(8,128)(2,1)} copy(bf16[20000,640]{0,1:T(8,128)(2,1)} %reshape.115) | data formatting | bytes 51200000 | tf_op jit(solution)/shard_map/reshape | solution.py:27
  1686.0 0.0 copy-done.5
  1686.0 0.1 broadcast_add_fusion.1
  1686.1 0.7 add.86
  1686.8 0.7 broadcast_add_fusion
  1687.5 1.8 iota_compare_fusion.5
  1689.3 0.0 all-to-all-done.2
  1689.3 66.1 %copy.41 = bf16[100,4,200,160]{2,1,3,0:T(4,128)(2,1)} copy(bf16[100,4,200,160]{0,3,2,1:T(8,128)(2,1)} %bitcast.7) | data formatting | bytes 51200000 | tf_op jit(solution)/shard_map/all_to_all | solution.py:31
  1755.4 22.7 %copy.34 = bf16[100,200,4,160]{1,3,2,0:T(8,128)(2,1)} copy(bf16[100,200,4,160]{1,2,3,0:T(4,128)(2,1)} %bitcast.22) | data formatting | bytes 51200000 | tf_op jit(solution)/shard_map/all_to_all | solution.py:31
  1778.1 45.9 %copy.35 = bf16[200,100,640]{2,1,0:T(8,128)(2,1)} copy(bf16[200,100,640]{0,2,1:T(8,128)(2,1)} %bitcast.23) | data formatting | bytes 51200000 | tf_op jit(solution)/shard_map/transpose | solution.py:32
  1824.0 32.6 %reshape.114 = bf16[20000,640]{1,0:T(8,128)(2,1)} reshape(bf16[200,100,640]{2,1,0:T(8,128)(2,1)} %copy.35) | data formatting | bytes 51200000 | tf_op jit(solution)/shard_map/reshape | solution.py:32
  1856.5 0.0 copy-start
  1856.5 0.0 all-gather.2.cloned.1.call-done
  1856.5 79.5 %convolution_convert_fusion = bf16[40000,1024]{1,0:T(8,128)(2,1)} fusion(bf16[1024,640]{0,1:T(8,128)(2,1)} %all-gather.2.cloned.1.call-done, bf16[20000,640]{1,0:T(8,128)(2,1)} %reshape.114, bf16[20000,640]{1,0:T(8,128)(2,1)} %copy.37), kind=kOutput, calls=%fused_computation.2 | convolution fusion | flops 52572160000 | bytes 134430720 | tf_op jit(solution)/shard_map/dot_general | solution.py:35
  1936.1 0.0 copy-done
  1936.1 69.4 %convert_add_fusion = f32[20000,1024]{1,0:T(8,128)} fusion(bf16[40000,1024]{1,0:T(8,128)(2,1)} %convolution_convert_fusion, pred[1024,1024]{1,0:T(32,128)(4,1)S(1)} %copy-done), kind=kOutput, calls=%fused_computation.1 | convolution fusion | flops 41984000000 | bytes 164888576 | tf_op jit(solution)/shard_map/dot_general | solution.py:44
  2005.5 0.0 copy-start.1
  2005.5 0.0 copy-start.3
  2005.5 72.3 %add.79 = f32[200,100,1024]{2,1,0:T(8,128)} reshape(f32[20000,1024]{1,0:T(8,128)} %convert_add_fusion) | data formatting | bytes 163840000 | tf_op jit(solution)/shard_map/add | solution.py:51
  2077.8 0.0 copy-done.1
  2077.8 0.0 copy-done.3
  2077.8 41.6 %divide_convert_fusion = bf16[200,100,1024]{2,1,0:T(8,128)(2,1)} fusion(f32[200,100,1024]{2,1,0:T(8,128)} %add.79, f32[1024]{0:T(1024)S(1)} %copy-done.3, f32[200,100]{1,0:T(8,128)S(1)} %copy-done.1), kind=kLoop, calls=%fused_computation | loop fusion | flops 61440000 | bytes 122964096 | tf_op jit(solution)/shard_map/convert_element_type | solution.py:51
  2119.4 28.8 %copy.36 = bf16[200,100,1024]{2,0,1:T(8,128)(2,1)} copy(bf16[200,100,1024]{2,1,0:T(8,128)(2,1)} %divide_convert_fusion) | data formatting | bytes 81920000 | tf_op jit(solution)/shard_map/convert_element_type | solution.py:51
  (1 shorter events, 0.0 us)
Async XLA Ops:
  6.5 46.0 %copy-start.4 = (s32[640]{0:T(1024)S(1)}, s32[640]{0:T(1024)}, u32[]{:S(2)}) copy-start(s32[640]{0:T(1024)} %param.9) | copy-start | bytes 7684
  1241.7 9.8 copy-start.2
  1241.7 447.6 %all-to-all-start.2 = ((bf16[100,800,160]{0,2,1:T(8,128)(2,1)}), bf16[100,800,160]{0,2,1:T(8,128)(2,1)}, u32[]{:S(2)}, u32[]{:S(2)}) async-start(bf16[100,800,160]{0,2,1:T(8,128)(2,1)} %bitcast.19), calls=%async_computation.2 | async-start | bytes 65536000 | tf_op jit(solution)/shard_map/all_to_all | solution.py:31
  1251.4 605.1 %all-gather.2.cloned.1.call-start = ((), (), s32[]{:S(2)}) async-start(), calls=%async_computation.3 | async-start | bytes 1474560 | tf_op jit(solution)/shard_map/all_gather | solution.py:37
  1610.0 76.0 %copy-start.5 = (f32[32]{0:T(128)S(1)}, f32[32]{0:T(128)}, u32[]{:S(2)}) copy-start(f32[32]{0:T(128)} %param.11) | copy-start | bytes 388
  1856.5 79.5 %copy-start = (pred[1024,1024]{1,0:T(32,128)(4,1)S(1)}, pred[1024,1024]{1,0:T(32,128)(4,1)}, u32[]{:S(2)}) copy-start(pred[1024,1024]{1,0:T(32,128)(4,1)} %iota_compare_fusion.5) | copy-start | bytes 3145732
  2005.5 72.3 %copy-start.1 = (f32[200,100]{1,0:T(8,128)S(1)}, f32[200,100]{1,0:T(8,128)}, u32[]{:S(2)}) copy-start(f32[200,100]{1,0:T(8,128)} %broadcast_add_fusion) | copy-start | bytes 240004
  2005.5 72.3 %copy-start.3 = (f32[1024]{0:T(1024)S(1)}, f32[1024]{0:T(1024)}, u32[]{:S(2)}) copy-start(f32[1024]{0:T(1024)} %add.86) | copy-start | bytes 12292
Sparse Core Ops, SparseCore 0:
  1610.1 21.1 all-gather.1
where the time goes:
time: 2160 us
  blocking collectives  1450 us (67%)
  local copies, waits for them, and re-layouts  467 us (22%)
  matrix products  149 us (7%)
  other arithmetic  67 us (3%)
    all_to_all x1, blocking collectives, per_device(): lax.all_to_all(first_move, 'col', split_axis=0, concat_axis=1, tiled=True)  717 us
    all_to_all x1, blocking collectives, per_device(): lax.all_to_all(masked, 'row', split_axis=2, concat_axis=0, tiled=True)  373 us
    all_gather x1, blocking collectives, per_device(): all_pairs = lax.all_gather(amplitudes, 'row', axis=0, tiled=True)  358 us
    all_to_all x2, local copies, waits for them, and re-layouts, per_device(): lax.all_to_all(second_move, 'row', split_axis=1, concat_axis=2, tiled=True)  88.8 us
    dot_general x1, matrix products, per_device(): lax.dot_general(stacked, lax.all_gather(all_pairs, 'col', axis=1, tiled=T...  79.5 us
    reshape x2, local copies, waits for them, and re-layouts, per_device(): flat = masked.reshape(tile_a * tile_b, slab)  74.5 us
    add x1, local copies, waits for them, and re-layouts, per_device(): return ((ladder.astype(jnp.float32) + other) / denom).astype(jnp.bfloat16)  72.3 us
    dot_general x1, matrix products, per_device(): jnp.dot(swapped, swapper, preferred_element_type=jnp.float32)  69.4 us
  transfers between devices with their start and end apart: 2, of which 0 were waited for; matrix products, arithmetic and copies ran while one was open for 11% of the time, Pallas kernels for 0%

commit v1 on v0

v1 whole, which is shorter than its diff:
```python
import functools

import jax
import jax.numpy as jnp
from jax import lax
from jax.experimental import pallas as pl
from jax.experimental.pallas import tpu as pltpu
from jax.sharding import PartitionSpec as P

LABELS = 8
LANES = 128


def round_up(value, step):
    return (value + step - 1) // step * step


def divisor_up_to(total, most):
    return max(n for n in range(1, most + 1) if total % n == 0)


def pack_kernel(lb_ref, shift_ref, la_ref, pair_ref, slot_ref, view_ref, own_ref, turned_ref, lhs, flat):
    count, eight, slab = view_ref.shape
    rows = turned_ref.shape[1]
    width = slot_ref.shape[1]

    @pl.when(pl.program_id(0) == 0)
    def _():
        flat[...] = jnp.zeros_like(flat)
        lhs[...] = jnp.zeros_like(lhs)

    pair = jnp.broadcast_to(pair_ref[...], (eight, slab))

    def one(b):
        run = jnp.bitwise_xor(la_ref[...], lb_ref[b])
        run = jnp.concatenate([run] * (slab // LANES), axis=1)
        return jnp.where(run == pair, view_ref[b].astype(jnp.float32), 0.0)

    def two(n, _):
        both = jnp.concatenate([one(2 * n), one(2 * n + 1)], axis=0)
        at = pl.multiple_of(2 * eight * n, 2 * eight)
        lhs[pl.ds(at, 2 * eight), :] = both.astype(lhs.dtype)
        return _

    lax.fori_loop(0, count // 2, two, None, unroll=5)
    if count % 2:
        last = jnp.concatenate([one(count - 1), jnp.zeros((eight, slab), jnp.float32)], axis=0)
        lhs[(count - 1) * eight : (count + 1) * eight, :] = last.astype(lhs.dtype)
    packed = jnp.dot(lhs[...], slot_ref[...], preferred_element_type=jnp.float32)
    for part in range(width // LANES):
        flat[part, : lhs.shape[0], :] = packed[:, part * LANES : (part + 1) * LANES]
    own_ref[...] = packed[: count * eight].reshape(count, eight, width).astype(own_ref.dtype)
    for j in range(eight):
        for part in range(width // LANES):
            column = pltpu.roll(flat[part, pl.ds(j, rows, stride=eight), :], shift_ref[0], 0)
            turned_ref[j, :, part * LANES : (part + 1) * LANES] = column.astype(turned_ref.dtype)


def pack(view, labels_a, labels_b, pair_irrep, slots, shift, padded_b, padded_a):
    tile_b, tile_a, slab = view.shape
    width = slots.shape[1]
    steps = pl.cdiv(tile_a, 8)
    spread = jnp.broadcast_to(jnp.pad(labels_a, (0, steps * 8 - tile_a))[:, None], (steps * 8, LANES))
    return pl.pallas_call(
        pack_kernel,
        grid_spec=pltpu.PrefetchScalarGridSpec(
            num_scalar_prefetch=2,
            grid=(steps,),
            in_specs=[
                pl.BlockSpec((8, LANES), lambda i, *_: (i, 0)),
                pl.BlockSpec((1, slab), lambda i, *_: (0, 0)),
                pl.BlockSpec((slab, width), lambda i, *_: (0, 0)),
                pl.BlockSpec((tile_b, 8, slab), lambda i, *_: (0, i, 0)),
            ],
            out_specs=[
                pl.BlockSpec((tile_b, 8, width), lambda i, *_: (0, i, 0)),
                pl.BlockSpec((8, padded_b, width), lambda i, *_: (i, 0, 0)),
            ],
            scratch_shapes=[
                pltpu.VMEM((round_up(tile_b, 2) * 8, slab), jnp.bfloat16),
                pltpu.VMEM((width // LANES, max(padded_b, round_up(tile_b, 2)) * 8, LANES), jnp.float32),
            ],
        ),
        out_shape=[
            jax.ShapeDtypeStruct((tile_b, padded_a, width), view.dtype),
            jax.ShapeDtypeStruct((tile_a, padded_b, width), view.dtype),
        ],
        compiler_params=pltpu.CompilerParams(vmem_limit_bytes=48 << 20),
        cost_estimate=pl.CostEstimate(
            flops=2 * tile_a * tile_b * slab * width,
            bytes_accessed=2 * tile_a * tile_b * (slab + 2 * width),
            transcendentals=0,
        ),
        name="pack",
    )(labels_b, shift, spread, pair_irrep[None, :], slots, view)


def ladder_kernel(
    bases, hops, where_ref, la_ref, lb_ref, vb_ref, spread_ref, va_ref, pe_ref, amp_ref, own_ref, *refs
):
    pieces, (out_ref, acc, mir_ref) = refs[:-3], refs[-3:]
    many, tile_a, pairs = out_ref.shape
    width = own_ref.shape[2]
    split = len(bases)
    inner = pl.num_programs(1)
    rows = pieces[0].shape[1]
    take = pl.ds(pl.program_id(1) * many, many)

    def assemble(hop, side):
        for part in range(split):
            piece = pieces[(side ^ part) * hops + hop]
            base = bases[part]
            shared = 0 if part == 0 else bases[part - 1] + rows - base
            if shared > 0:
                both = mir_ref[:, base : base + shared, :].astype(jnp.float32)
                both = both + piece[take, :shared, :].astype(jnp.float32)
                mir_ref[:, base : base + shared, :] = both.astype(mir_ref.dtype)
            mir_ref[:, base + shared : base + rows, :] = piece[take, shared:, :]

    for hop in range(hops):
        for side in range(split):
            pl.when(jnp.logical_and(pl.program_id(0) == hop, where_ref[1] == side))(
                functools.partial(assemble, hop, side)
            )
    first = (jnp.bitwise_xor(pl.program_id(0), where_ref[0]) * inner + pl.program_id(1)) * many
    b_low = lb_ref[first]
    b_high = lb_ref[first + many - 1]

    def tile(at, size):
        own = own_ref[:, pl.ds(at, 16), :].reshape(many * 16, width)
        mir = mir_ref[:, pl.ds(at, 16), :].reshape(many * 16, width)
        lhs = jnp.concatenate([own, mir], axis=1)
        a_low = la_ref[at]
        a_high = la_ref[at + size - 1]
        single = jnp.logical_and(a_low == a_high, b_low == b_high)

        @pl.when(single)
        def _():
            acc[...] = jnp.dot(lhs, amp_ref[jnp.bitwise_xor(a_low, b_low)], preferred_element_type=jnp.float32)

        @pl.when(jnp.logical_not(single))
        def _():
            acc[...] = jnp.zeros_like(acc)
            spread = spread_ref[pl.ds(at, 16), :]

            def over_a(label_a, _):
                def over_b(label_b, _):
                    keep = [
                        jnp.where(lb_ref[first + b] == label_b, spread, -1) == label_a for b in range(many)
                    ]
                    keep = jnp.concatenate(keep, axis=0)
                    keep = jnp.concatenate([keep.astype(jnp.float32)] * (2 * width // LANES), axis=1)
                    part = jnp.where(keep > 0, lhs.astype(jnp.float32), 0.0).astype(lhs.dtype)
                    acc[...] += jnp.dot(
                        part, amp_ref[jnp.bitwise_xor(label_a, label_b)], preferred_element_type=jnp.float32
                    )
                    return _

                return lax.fori_loop(b_low, b_high + 1, over_b, _)

            lax.fori_loop(a_low, a_high + 1, over_a, None)

        energy_a = va_ref[pl.ds(at, 16), :]
        for b in range(many):
            level = energy_a + vb_ref[first + b]
            level = jnp.concatenate([level] * (pairs // LANES), axis=1)
            denom = level - pe_ref[...]
            value = (acc[16 * b : 16 * b + 16, :] / denom).astype(out_ref.dtype)
            out_ref[b, pl.ds(at, size), :] = value[:size]

    whole = tile_a // 16

    def step(n, _):
        tile(pl.multiple_of(16 * n, 16), 16)
        return _

    lax.fori_loop(0, whole, step, None)
    if tile_a % 16:
        tile(whole * 16, tile_a % 16)


def ladder(own, pieces, hops, bases, where, amps, labels_a, labels_b, energy_a, energy_b, pair_energy, tile_a):
    tile_b, padded_a, width = own.shape
    pairs = amps.shape[2]
    run = tile_b // hops
    many = divisor_up_to(run, 25 if width <= LANES else 5)
    inner = run // many
    pad = (0, padded_a - tile_a)
    spread = jnp.broadcast_to(jnp.pad(labels_a, pad)[:, None], (padded_a, LANES))
    spread_energy = jnp.broadcast_to(jnp.pad(energy_a, pad)[:, None], (padded_a, LANES))
    once = pl.Buffered(1)

    def block(i, n, where_ref, *_):
        return (jnp.bitwise_xor(i, where_ref[0]) * inner + n, 0, 0)

    return pl.pallas_call(
        functools.partial(ladder_kernel, bases, hops),
        grid_spec=pltpu.PrefetchScalarGridSpec(
            num_scalar_prefetch=4,
            grid=(hops, inner),
            in_specs=[
                pl.BlockSpec((padded_a, LANES), lambda *_: (0, 0)),
                pl.BlockSpec((padded_a, LANES), lambda *_: (0, 0)),
                pl.BlockSpec((1, pairs), lambda *_: (0, 0)),
                pl.BlockSpec(amps.shape, lambda *_: (0, 0, 0), pipeline_mode=once),
                pl.BlockSpec((many, padded_a, width), block),
            ]
            + [pl.BlockSpec(piece.shape, lambda *_: (0, 0, 0), pipeline_mode=once) for piece in pieces],
            out_specs=pl.BlockSpec((many, tile_a, pairs), block),
            scratch_shapes=[
                pltpu.VMEM((many * 16, pairs), jnp.float32),
                pltpu.VMEM((many, padded_a, width), own.dtype),
            ],
        ),
        out_shape=jax.ShapeDtypeStruct((tile_b, tile_a, pairs), own.dtype),
        compiler_params=pltpu.CompilerParams(vmem_limit_bytes=60 << 20),
        cost_estimate=pl.CostEstimate(
            flops=4 * tile_a * tile_b * width * pairs,
            bytes_accessed=2 * tile_a * tile_b * (2 * width + pairs),
            transcendentals=0,
        ),
        name="ladder",
    )(where, labels_a, labels_b, energy_b, spread, spread_energy, pair_energy[None, :], amps, own, *pieces)


def pair_swapper(occupied):
    pairs = occupied * occupied
    source = jnp.arange(pairs, dtype=jnp.int32)
    target = source % occupied * occupied + source // occupied
    return (source[:, None] == target[None, :]).astype(jnp.bfloat16)


def per_device(rows, cols, integrals, amplitudes, virt_irrep, pair_irrep, virt_energy, occ_energy):
    tile_a, tile_b, slab = integrals.shape
    occupied = occ_energy.shape[0]
    pairs = occupied * occupied
    split = cols // rows
    row_at = lax.axis_index("row")
    col_at = lax.axis_index("col")
    labels_a = lax.dynamic_slice_in_dim(virt_irrep, row_at * tile_a, tile_a, 0)
    labels_b = lax.dynamic_slice_in_dim(virt_irrep, col_at * tile_b, tile_b, 0)
    energy_a = lax.dynamic_slice_in_dim(virt_energy, row_at * tile_a, tile_a, 0)
    energy_b = lax.dynamic_slice_in_dim(virt_energy, col_at * tile_b, tile_b, 0)
    pair_energy = (occ_energy[:, None] + occ_energy[None, :]).reshape(pairs)

    labels = jnp.arange(LABELS, dtype=jnp.int32)
    member = pair_irrep[None, :] == labels[:, None]
    widths = jnp.sum(member.astype(jnp.int32), axis=1)
    starts = jnp.sum((pair_irrep[None, :] < labels[:, None]).astype(jnp.int32), axis=1)
    place = jnp.arange(slab, dtype=jnp.int32) - jnp.sum(jnp.where(member, starts[:, None], 0), axis=0)

    bases = [part * tile_b // 16 * 16 for part in range(split)]
    shifts = [part * tile_b - base for part, base in enumerate(bases)]
    padded_b = round_up(max(shifts) + tile_b, 8)
    padded_a = round_up(max(tile_a, bases[-1] + padded_b), 16)
    shift = jnp.asarray(shifts, jnp.int32)[col_at % split][None]
    view = jnp.transpose(integrals, (1, 0, 2))

    side = col_at % split
    layer = col_at // split
    spreads = cols == rows * split and rows & (rows - 1) == 0 and tile_b % rows == 0

    def move(piece, goal):
        moves = []
        for r in range(rows):
            for c in range(cols):
                to_row, to_layer, to_side = goal(r, c // split, c % split)
                moves.append((r * cols + c, to_row * cols + to_layer * split + to_side))
        return lax.ppermute(piece, ("row", "col"), moves)

    def exchange(turned, hops, apart):
        shape = (split, hops, tile_b // hops) + turned.shape[1:]
        turned = turned.reshape(shape)
        pieces, before = [], None
        for flip in range(split):
            part = lax.dynamic_index_in_dim(turned, jnp.bitwise_xor(side, flip), 0, keepdims=False)
            if hops == 1:
                pieces.append(move(part[0], lambda r, z, k: (z, r, k ^ flip)))
                continue
            chunks = [part[n] for n in range(hops)]
            if before is not None:
                chunks = lax.optimization_barrier((chunks, before))[0]
            first = [chunks[0]] + [
                move(chunks[n], lambda r, z, k, n=n: (r ^ n, z, k)) for n in range(1, hops)
            ]
            before = first[1:]
            ready = [lax.select_n(jnp.bitwise_xor(apart, n), *first) for n in range(hops)]
            second = [ready[0]] + [
                move(ready[n], lambda r, z, k, n=n: (r, z ^ n, k)) for n in range(1, hops)
            ]
            ready = [lax.select_n(jnp.bitwise_xor(apart, n), *second) for n in range(hops)]
            for n in range(hops):
                if n == 0 and flip == 0:
                    pieces.append(ready[n])
                else:
                    pieces.append(move(ready[n], lambda r, z, k, n=n: (r ^ n, z, k ^ flip)))
        return pieces

    def run(width, hops):
        apart = jnp.bitwise_xor(row_at, layer) if hops > 1 else jnp.int32(0)
        slots = (place[:, None] == jnp.arange(width, dtype=jnp.int32)[None, :]).astype(integrals.dtype)
        own, turned = pack(view, labels_a, labels_b, pair_irrep, slots, shift, padded_b, padded_a)
        pieces = exchange(turned, hops, apart)
        depth, share = amplitudes.shape[1], amplitudes.shape[0]
        gathered = lax.all_gather(amplitudes.T, ("row", "col"), axis=0)
        gathered = gathered.reshape(rows, cols, depth, share).transpose(1, 2, 0, 3).reshape(slab, pairs)
        swapped = jnp.dot(gathered, pair_swapper(occupied), preferred_element_type=jnp.float32).astype(
            gathered.dtype
        )
        both = jnp.pad(jnp.stack([gathered, swapped]), ((0, 0), (0, width), (0, 0)))
        amps = jnp.stack(
            [lax.dynamic_slice(both, (0, starts[g], 0), (2, width, pairs)) for g in range(LABELS)]
        ).reshape(LABELS, 2 * width, pairs)
        where = jnp.stack([apart, side])
        return ladder(own, pieces, hops, bases, where, amps, labels_a, labels_b, energy_a, energy_b, pair_energy, tile_a)

    widest = jnp.max(widths)
    out = lax.cond(
        widest <= LANES, lambda: run(LANES, rows if spreads else 1), lambda: run(3 * LANES, 1)
    )
    return jnp.transpose(out, (1, 0, 2))


def solution(mesh):
    rows, cols = mesh.shape["row"], mesh.shape["col"]
    return jax.shard_map(
        functools.partial(per_device, rows, cols),
        mesh=mesh,
        in_specs=(P("row", "col", None), P("row", "col"), P(), P(), P(), P()),
        out_specs=P("row", "col", None),
        check_vma=False,
    )
```

time: 2160 us -> 316 us (0.15)
  blocking collectives: 1450 us -> 0 us
  local copies, waits for them, and re-layouts: 467 us -> 25.7 us
  matrix products: 149 us -> 1.6 us
  waiting for transfers between devices: 0.02 us -> 127 us
  Pallas kernels: 0 us -> 83.2 us
  other arithmetic: 67 us -> 20.1 us
    all_to_all x2 -> x0, blocking collectives: 1090 us -> none  [the longest x1 717 us: per_device(): lax.all_to_all(first_move, 'col', split_axis=0, concat_axis=1, tiled=True)]
    all_gather x1 -> x0, blocking collectives: 358 us -> none  [per_device(): all_pairs = lax.all_gather(amplitudes, 'row', axis=0, tiled=True)]
    all_to_all x4 -> x0, local copies, waits for them, and re-layouts: 164 us -> none  [the longest x2 88.8 us: per_device(): lax.all_to_all(second_move, 'row', split_axis=1, concat_axis=2, tiled=True)]
    dot_general x2 -> x1, matrix products: 149 us -> 1.6 us  [run(): jnp.dot(gathered, pair_swapper(occupied), preferred_element_type=jnp.floa...]
    ppermute x0 -> x19, waiting for transfers between devices: none -> 127 us  [move(): return lax.ppermute(piece, ('row', 'col'), moves)]
    reshape x3 -> x1, local copies, waits for them, and re-layouts: 107 us -> 1.18 us  [run(): both = jnp.pad(jnp.stack([gathered, swapped]), ((0, 0), (0, width), (0, 0)))]
    pallas_call x0 -> x2, Pallas kernels: none -> 83.2 us  [the longest x1 52.7 us: ladder(): pl.pallas_call(functools.partial(ladder_kernel, bases, hops), grid_spec=p...]
    add x2 -> x0, local copies, waits for them, and re-layouts: 73 us -> none  [the longest x1 72.3 us: per_device(): return ((ladder.astype(jnp.float32) + other) / denom).astype(jnp.bfloat16)]
  transfers between devices with their start and end apart: 2 -> 20, of which waited for: 0 -> 8; matrix products, arithmetic and copies ran while one was open for 11% -> 10% of each run, Pallas kernels for 0% -> 0%
where the time goes in v1:
time: 316 us; the launch traced here: 312 us
  waiting for transfers between devices  127 us (40%)
  Pallas kernels  83.2 us (26%)
  local copies, waits for them, and re-layouts  25.7 us (8%)
  starting transfers between devices  25.5 us (8%)
  other arithmetic  20.1 us (6%)
  loops' own time  15 us (5%)
  between operations  14 us (4%)
    ppermute x19, waiting for transfers between devices, move(): return lax.ppermute(piece, ('row', 'col'), moves)  127 us
    pallas_call x1, Pallas kernels, ladder(): pl.pallas_call(functools.partial(ladder_kernel, bases, hops), grid_spec=p...  52.7 us
    pallas_call x1, Pallas kernels, pack(): pl.pallas_call(pack_kernel, grid_spec=pltpu.PrefetchScalarGridSpec(num_sc...  30.5 us
    ppermute x19, starting transfers between devices, move(): return lax.ppermute(piece, ('row', 'col'), moves)  25.4 us
    another operation x1, loops' own time, per_device(): lax.cond(widest <= LANES, lambda: run(LANES, rows if spreads else 1), lam...  15 us
    select_n x4, other arithmetic, exchange(): lax.select_n(jnp.bitwise_xor(apart, n), *second)  10.9 us
  transfers between devices with their start and end apart: 20, of which 8 were waited for; matrix products, arithmetic and copies ran while one was open for 10% of the time, Pallas kernels for 0%

profile of v1, /device:TPU:0, one launch (start us, length us, event | category | flops | bytes accessed | tf_op | source)
XLA Modules:
  0.0 311.9 jit_solution(18361232128123129198)
XLA Ops:
  6.5 0.8 convert_reduce_fusion
  7.3 0.8 dynamic_slice.79
  8.1 0.8 dynamic_slice.81
  8.9 0.8 dynamic_slice.77
  9.6 0.8 dynamic_slice.78
  10.4 0.9 select_reduce_fusion
  11.3 0.6 reduce_max.9
  12.6 0.8 broadcast_add_fusion
  13.4 291.7 %conditional.1 = (bf16[100,200,1024]{2,1,0:T(8,128)(2,1)}) conditional(s32[]{:T(128)} %convert_element_type.37, (s32[]{:T(128)}, s32[200]{0:T(256)S(1)}, f32[200]{0:T(256)S(1)}, f32[32,32]{1,0:T(8,128)S(1)}, bf16[256,80]{0,1:T(8,128)(2,1)}, /*index=5*/s32[8]{0:T(128)S(1)}, s32[640]{0:T(1024)}, s32[640]{0:T(1024)S(1)}, s32[100]{0:T(128)S(1)}, ...), branch_computations={%region_4.5_spmd, %region_5.6_spmd} | conditional | flops 42646749184 | bytes 346703584 | solution.py:318
  13.4 0.1 all-gather.7.cloned.1.call-start
  13.5 0.7 broadcast_in_dim.25.pair_ref
  14.2 0.1 fusion.24.slot_ref
  14.3 0.1 broadcast_in_dim.24.la_ref
  14.4 30.5 %pack.3 = (bf16[100,208,128]{2,1,0:T(8,128)(2,1)S(1)}, bf16[200,104,128]{2,1,0:T(8,128)(2,1)}) custom-call(s32[100]{0:T(128)S(1)} %get-tuple-element.106.lb_ref, s32[1]{0:T(128)} %get-tuple-element.112.shift_ref, s32[200,128]{1,0:T(8,128)S(1)} %broadcast_in_dim.24.la_ref, s32[1,640]{1,0:T(1,128)S(1)} %broadcast_in_dim.25.pair_ref, ...), custom_call_target="tpu_custom_call" | custom-call | flops 3276800000 | bytes 35840000 | tf_op jit(solution)/shard_map/cond/branch_1_fun/pack/pallas_call | solution.py:64
  45.0 6.1 %dynamic-slice_bitcast_fusion.2 = (bf16[25,104,128]{2,1,0:T(8,128)(2,1)}, bf16[25,104,128]{2,1,0:T(8,128)(2,1)}, bf16[25,104,128]{2,1,0:T(8,128)(2,1)}, bf16[25,...) fusion(bf16[2,4,25,104,128]{4,3,2,1,0:T(8,128)(2,1)} %bitcast.1, ...), kind=kLoop, calls=%fused_computation.52 | loop fusion | bytes 9318420 | tf_op jit(solution)/shard_map/cond/branch_1_fun/squeeze | solution.py:280
  51.0 3.0 collective-permute-start.3
  54.0 1.5 collective-permute-start.2
  55.6 13.4 %collective-permute-done.3 = bf16[25,104,128]{2,1,0:T(8,128)(2,1)S(1)} collective-permute-done((bf16[25,104,128]{2,1,0:T(8,128)(2,1)S(1)}, bf16[25,104,128]{2,1,0:T(8,128)(2,1)S(1)}, u32[]{:S(2)}, u32[]{:S(2)}) %collective-permute-start.3) | collective-permute-done | bytes 665632 | tf_op jit(solution)/shard_map/cond/branch_1_fun/ppermute | solution.py:269
  69.0 2.9 collective-permute-done.2
  71.8 12.6 %collective-permute-done.4 = bf16[25,104,128]{2,1,0:T(8,128)(2,1)S(1)} collective-permute-done((bf16[25,104,128]{2,1,0:T(8,128)(2,1)S(1)}, bf16[25,104,128]{2,1,0:T(8,128)(2,1)S(1)}, u32[]{:S(2)}, u32[]{:S(2)}) %collective-permute-start.4) | collective-permute-done | bytes 665632 | tf_op jit(solution)/shard_map/cond/branch_1_fun/ppermute | solution.py:269
  84.5 1.6 collective-permute-start.11
  86.2 1.6 collective-permute-start.12
  87.8 0.3 collective-permute-start.13
  88.1 3.0 select_select_fusion.14
  91.1 1.7 collective-permute-start.5
  92.8 2.5 collective-permute-start.7
  95.3 7.5 %collective-permute-done.11 = bf16[25,104,128]{2,1,0:T(8,128)(2,1)S(1)} collective-permute-done((bf16[25,104,128]{2,1,0:T(8,128)(2,1)}, bf16[25,104,128]{2,1,0:T(8,128)(2,1)S(1)}, u32[]{:S(2)}, u32[]{:S(2)}) %collective-permute-start.11) | collective-permute-done | bytes 665632 | tf_op jit(solution)/shard_map/cond/branch_1_fun/ppermute | solution.py:269
  102.8 2.7 collective-permute-start.6
  105.6 0.7 fusion.35
  116.1 0.7 broadcast_in_dim_reshape.5.pe_ref
  121.7 0.6 pad_add_fusion.1.where_ref
  122.3 2.0 select_select_fusion.6
  124.3 1.6 collective-permute-start.14
  126.0 1.8 collective-permute-start.15
  127.9 61.2 %collective-permute-done.6 = bf16[25,104,128]{2,1,0:T(8,128)(2,1)} collective-permute-done((bf16[25,104,128]{2,1,0:T(8,128)(2,1)}, bf16[25,104,128]{2,1,0:T(8,128)(2,1)}, u32[]{:S(2)}, u32[]{:S(2)}) %collective-permute-start.6) | collective-permute-done | bytes 665632 | tf_op jit(solution)/shard_map/cond/branch_1_fun/ppermute | solution.py:269
  189.1 3.1 select_select_fusion.8
  192.1 3.3 %select_select_fusion.9 = (bf16[25,104,128]{2,1,0:T(8,128)(2,1)}, bf16[25,104,128]{2,1,0:T(8,128)(2,1)}, bf16[25,104,128]{2,1,0:T(8,128)(2,1)}) fusion(bf16[25,104,128]{2,1,0:T(8,128)(2,1)} %collective-permute-done.6, bf16[25,104,128]{2,1,0:T(8,128)(2,1)} %collective-permute-done.7, bf16[25,104,128]{2,1,0:T(8,128)(2,1)S(1)} %get-tuple-element.156, ...), kind=kLoop, calls=%fused_computation.69 | loop fusion | flops 2995200 | bytes 4659209 | tf_op jit(solution)/shard_map/cond/branch_1_fun/select_n | solution.py:291
  195.5 1.5 collective-permute-start.9
  197.0 1.3 collective-permute-start.8
  198.3 0.7 collective-permute-start.10
  199.0 15.4 %collective-permute-done.15 = bf16[25,104,128]{2,1,0:T(8,128)(2,1)S(1)} collective-permute-done((bf16[25,104,128]{2,1,0:T(8,128)(2,1)S(1)}, bf16[25,104,128]{2,1,0:T(8,128)(2,1)S(1)}, u32[]{:S(2)}, u32[]{:S(2)}) %collective-permute-start.15) | collective-permute-done | bytes 665632 | tf_op jit(solution)/shard_map/cond/branch_1_fun/ppermute | solution.py:269
  214.4 2.6 select_select_fusion
  217.0 1.9 select_select_fusion.1
  218.9 2.8 collective-permute-start.18
  221.7 2.3 copy.28
  224.0 1.2 reshape.129
  225.2 0.3 copy.31
  225.5 1.6 fusion.23
  227.1 0.3 fusion.20
  227.4 2.4 constant_dynamic-slice_fusion.8
  229.8 0.8 bitcast_dynamic-update-slice_fusion.15
  230.6 0.8 bitcast_dynamic-update-slice_fusion.14
  231.6 0.5 collective-permute-start.20
  232.1 0.8 bitcast_dynamic-update-slice_fusion.13
  232.9 0.8 bitcast_dynamic-update-slice_fusion.12
  233.7 0.9 bitcast_dynamic-update-slice_fusion.11
  234.6 0.9 bitcast_dynamic-update-slice_fusion.10
  235.5 0.9 bitcast_dynamic-update-slice_fusion.9
  236.3 0.8 bitcast_dynamic-update-slice_fusion.8.amp_ref
  237.2 0.1 collective-permute-done.18.refs_5_
  237.3 13.5 %collective-permute-done.20.refs_7_ = bf16[25,104,128]{2,1,0:T(8,128)(2,1)S(1)} collective-permute-done((bf16[25,104,128]{2,1,0:T(8,128)(2,1)S(1)}, bf16[25,104,128]{2,1,0:T(8,128)(2,1)S(1)}, u32[]{:S(2)}, u32[]{:S(2)}) %collective-permute-start.20) | collective-permute-done | bytes 665632 | tf_op jit(solution)/shard_map/cond/branch_1_fun/ppermute | solution.py:269
  250.8 0.8 broadcast_in_dim.22.spread_ref
  251.6 0.7 broadcast_in_dim.23.va_ref
  252.4 52.7 %ladder.3 = bf16[100,200,1024]{2,1,0:T(8,128)(2,1)} custom-call(s32[2]{0:T(128)} %pad_add_fusion.1.where_ref, s32[200]{0:T(256)S(1)} %get-tuple-element.105.la_ref, s32[100]{0:T(128)S(1)} %get-tuple-element.106.lb_ref, f32[100]{0:T(128)S(1)} %get-tuple-element.107.vb_ref, s32[208,128]{1,0:T(8,128)} %broadcast_in_dim.22.spread_ref, ...), custom_call_target="tpu_custom_call" | custom-call | flops 10485760000 | bytes 51200000 | tf_op jit(solution)/shard_map/cond/branch_1_fun/ladder/pallas_call | solution.py:196
  (33 shorter events, 0.3 us)
Async XLA Ops:
  13.4 208.3 %all-gather.7.cloned.1.call-start = ((), (), s32[]{:S(2)}) async-start(), calls=%async_computation.1 | async-start | bytes 1351680 | tf_op jit(solution)/shard_map/cond/branch_1_fun/all_gather | solution.py:305
  44.9 6.1 %copy-start = (bf16[100,208,128]{2,1,0:T(8,128)(2,1)}, bf16[100,208,128]{2,1,0:T(8,128)(2,1)S(1)}, u32[]{:S(2)}) copy-start(bf16[100,208,128]{2,1,0:T(8,128)(2,1)S(1)} %get-tuple-element.116.own_ref) | copy-start | bytes 15974404 | tf_op jit(solution)/shard_map/cond
  51.0 17.9 %collective-permute-start.3 = (bf16[25,104,128]{2,1,0:T(8,128)(2,1)S(1)}, bf16[25,104,128]{2,1,0:T(8,128)(2,1)S(1)}, u32[]{:S(2)}, u32[]{:S(2)}) collective-permute-start(bf16[25,104,128]{2,1,0:T(8,128)(2,1)S(1)} %get-tuple-element.182), channel_id=1, source_target_pairs={{0,16},{1,17},{2,18},{3,19},{4,20},{5,21},{6,22},{7,23},{8,24},{9,... | collective-permute-start | bytes 1996808 | tf_op jit(solution)/shard_map/cond/branch_1_fun/ppermute | solution.py:269
  54.0 17.8 %collective-permute-start.2 = (bf16[25,104,128]{2,1,0:T(8,128)(2,1)S(1)}, bf16[25,104,128]{2,1,0:T(8,128)(2,1)S(1)}, u32[]{:S(2)}, u32[]{:S(2)}) collective-permute-start(bf16[25,104,128]{2,1,0:T(8,128)(2,1)S(1)} %get-tuple-element.183), channel_id=1, source_target_pairs={{0,8},{1,9},{2,10},{3,11},{4,12},{5,13},{6,14},{7,15},{8,0},{9,1},... | collective-permute-start | bytes 1996808 | tf_op jit(solution)/shard_map/cond/branch_1_fun/ppermute | solution.py:269
  55.5 29.0 %collective-permute-start.4 = (bf16[25,104,128]{2,1,0:T(8,128)(2,1)S(1)}, bf16[25,104,128]{2,1,0:T(8,128)(2,1)S(1)}, u32[]{:S(2)}, u32[]{:S(2)}) collective-permute-start(bf16[25,104,128]{2,1,0:T(8,128)(2,1)S(1)} %get-tuple-element.184), channel_id=1, source_target_pairs={{0,24},{1,25},{2,26},{3,27},{4,28},{5,29},{6,30},{7,31},{8,16},{9,... | collective-permute-start | bytes 1996808 | tf_op jit(solution)/shard_map/cond/branch_1_fun/ppermute | solution.py:269
  84.5 18.3 %collective-permute-start.11 = (bf16[25,104,128]{2,1,0:T(8,128)(2,1)}, bf16[25,104,128]{2,1,0:T(8,128)(2,1)S(1)}, u32[]{:S(2)}, u32[]{:S(2)}) collective-permute-start(bf16[25,104,128]{2,1,0:T(8,128)(2,1)} %get-tuple-element.119), channel_id=1, source_target_pairs={{0,8},{1,9},{2,10},{3,11},{4,12},{5,13},{6,14},{7,15},{8,0},{9,1},... | collective-permute-start | bytes 1996808 | tf_op jit(solution)/shard_map/cond/branch_1_fun/ppermute | solution.py:269
  86.2 36.1 %collective-permute-start.12 = (bf16[25,104,128]{2,1,0:T(8,128)(2,1)}, bf16[25,104,128]{2,1,0:T(8,128)(2,1)}, u32[]{:S(2)}, u32[]{:S(2)}) collective-permute-start(bf16[25,104,128]{2,1,0:T(8,128)(2,1)} %get-tuple-element.120), channel_id=1, source_target_pairs={{0,16},{1,17},{2,18},{3,19},{4,20},{5,21},{6,22},{7,23},{8,24},{9,... | collective-permute-start | bytes 1996808 | tf_op jit(solution)/shard_map/cond/branch_1_fun/ppermute | solution.py:269
  87.8 34.5 %collective-permute-start.13 = (bf16[25,104,128]{2,1,0:T(8,128)(2,1)}, bf16[25,104,128]{2,1,0:T(8,128)(2,1)}, u32[]{:S(2)}, u32[]{:S(2)}) collective-permute-start(bf16[25,104,128]{2,1,0:T(8,128)(2,1)} %get-tuple-element.121), channel_id=1, source_target_pairs={{0,24},{1,25},{2,26},{3,27},{4,28},{5,29},{6,30},{7,31},{8,16},{9,... | collective-permute-start | bytes 1996808 | tf_op jit(solution)/shard_map/cond/branch_1_fun/ppermute | solution.py:269
  91.1 34.9 %collective-permute-start.5 = (bf16[25,104,128]{2,1,0:T(8,128)(2,1)}, bf16[25,104,128]{2,1,0:T(8,128)(2,1)}, u32[]{:S(2)}, u32[]{:S(2)}) collective-permute-start(bf16[25,104,128]{2,1,0:T(8,128)(2,1)} %get-tuple-element.175), channel_id=1, source_target_pairs={{0,2},{1,3},{2,0},{3,1},{4,6},{5,7},{6,4},{7,5},{8,10},{9,11},{10,... | collective-permute-start | bytes 1996808 | tf_op jit(solution)/shard_map/cond/branch_1_fun/ppermute | solution.py:269
  92.8 35.0 %collective-permute-start.7 = (bf16[25,104,128]{2,1,0:T(8,128)(2,1)}, bf16[25,104,128]{2,1,0:T(8,128)(2,1)}, u32[]{:S(2)}, u32[]{:S(2)}) collective-permute-start(bf16[25,104,128]{2,1,0:T(8,128)(2,1)} %get-tuple-element.176), channel_id=1, source_target_pairs={{0,6},{1,7},{2,4},{3,5},{4,2},{5,3},{6,0},{7,1},{8,14},{9,15},{10,... | collective-permute-start | bytes 1996808 | tf_op jit(solution)/shard_map/cond/branch_1_fun/ppermute | solution.py:269
  102.8 86.3 %collective-permute-start.6 = (bf16[25,104,128]{2,1,0:T(8,128)(2,1)}, bf16[25,104,128]{2,1,0:T(8,128)(2,1)}, u32[]{:S(2)}, u32[]{:S(2)}) collective-permute-start(bf16[25,104,128]{2,1,0:T(8,128)(2,1)} %get-tuple-element.177), channel_id=1, source_target_pairs={{0,4},{1,5},{2,6},{3,7},{4,0},{5,1},{6,2},{7,3},{8,12},{9,13},{10,... | collective-permute-start | bytes 1996808 | tf_op jit(solution)/shard_map/cond/branch_1_fun/ppermute | solution.py:269
  124.3 74.0 %collective-permute-start.14 = (bf16[25,104,128]{2,1,0:T(8,128)(2,1)S(1)}, bf16[25,104,128]{2,1,0:T(8,128)(2,1)S(1)}, u32[]{:S(2)}, u32[]{:S(2)}) collective-permute-start(bf16[25,104,128]{2,1,0:T(8,128)(2,1)S(1)} %get-tuple-element.196), channel_id=1, source_target_pairs={{0,2},{1,3},{2,0},{3,1},{4,6},{5,7},{6,4},{7,5},{8,10},{9,11},{10,... | collective-permute-start | bytes 1996808 | tf_op jit(solution)/shard_map/cond/branch_1_fun/ppermute | solution.py:269
  125.9 73.0 %collective-permute-start.16 = (bf16[25,104,128]{2,1,0:T(8,128)(2,1)S(1)}, bf16[25,104,128]{2,1,0:T(8,128)(2,1)S(1)}, u32[]{:S(2)}, u32[]{:S(2)}) collective-permute-start(bf16[25,104,128]{2,1,0:T(8,128)(2,1)S(1)} %get-tuple-element.197), channel_id=1, source_target_pairs={{0,6},{1,7},{2,4},{3,5},{4,2},{5,3},{6,0},{7,1},{8,14},{9,15},{10,... | collective-permute-start | bytes 1996808 | tf_op jit(solution)/shard_map/cond/branch_1_fun/ppermute | solution.py:269
  126.0 88.4 %collective-permute-start.15 = (bf16[25,104,128]{2,1,0:T(8,128)(2,1)S(1)}, bf16[25,104,128]{2,1,0:T(8,128)(2,1)S(1)}, u32[]{:S(2)}, u32[]{:S(2)}) collective-permute-start(bf16[25,104,128]{2,1,0:T(8,128)(2,1)S(1)} %get-tuple-element.198), channel_id=1, source_target_pairs={{0,4},{1,5},{2,6},{3,7},{4,0},{5,1},{6,2},{7,3},{8,12},{9,13},{10,... | collective-permute-start | bytes 1996808 | tf_op jit(solution)/shard_map/cond/branch_1_fun/ppermute | solution.py:269
  195.5 36.0 %collective-permute-start.9 = (bf16[25,104,128]{2,1,0:T(8,128)(2,1)}, bf16[25,104,128]{2,1,0:T(8,128)(2,1)S(1)}, u32[]{:S(2)}, u32[]{:S(2)}) collective-permute-start(bf16[25,104,128]{2,1,0:T(8,128)(2,1)} %get-tuple-element.199), channel_id=1, source_target_pairs={{0,16},{1,17},{2,18},{3,19},{4,20},{5,21},{6,22},{7,23},{8,24},{9,... | collective-permute-start | bytes 1996808 | tf_op jit(solution)/shard_map/cond/branch_1_fun/ppermute | solution.py:269
  197.0 34.5 %collective-permute-start.8 = (bf16[25,104,128]{2,1,0:T(8,128)(2,1)}, bf16[25,104,128]{2,1,0:T(8,128)(2,1)}, u32[]{:S(2)}, u32[]{:S(2)}) collective-permute-start(bf16[25,104,128]{2,1,0:T(8,128)(2,1)} %get-tuple-element.200), channel_id=1, source_target_pairs={{0,8},{1,9},{2,10},{3,11},{4,12},{5,13},{6,14},{7,15},{8,0},{9,1},... | collective-permute-start | bytes 1996808 | tf_op jit(solution)/shard_map/cond/branch_1_fun/ppermute | solution.py:269
  198.3 38.8 %collective-permute-start.10 = (bf16[25,104,128]{2,1,0:T(8,128)(2,1)}, bf16[25,104,128]{2,1,0:T(8,128)(2,1)}, u32[]{:S(2)}, u32[]{:S(2)}) collective-permute-start(bf16[25,104,128]{2,1,0:T(8,128)(2,1)} %get-tuple-element.155), channel_id=1, source_target_pairs={{0,24},{1,25},{2,26},{3,27},{4,28},{5,29},{6,30},{7,31},{8,16},{9,... | collective-permute-start | bytes 1996808 | tf_op jit(solution)/shard_map/cond/branch_1_fun/ppermute | solution.py:269
  218.9 18.3 %collective-permute-start.19 = (bf16[25,104,128]{2,1,0:T(8,128)(2,1)}, bf16[25,104,128]{2,1,0:T(8,128)(2,1)}, u32[]{:S(2)}, u32[]{:S(2)}) collective-permute-start(bf16[25,104,128]{2,1,0:T(8,128)(2,1)} %get-tuple-element.193), channel_id=1, source_target_pairs={{0,17},{1,16},{2,19},{3,18},{4,21},{5,20},{6,23},{7,22},{8,25},{9,... | collective-permute-start | bytes 1996808 | tf_op jit(solution)/shard_map/cond/branch_1_fun/ppermute | solution.py:269
  218.9 18.4 %collective-permute-start.18 = (bf16[25,104,128]{2,1,0:T(8,128)(2,1)}, bf16[25,104,128]{2,1,0:T(8,128)(2,1)}, u32[]{:S(2)}, u32[]{:S(2)}) collective-permute-start(bf16[25,104,128]{2,1,0:T(8,128)(2,1)} %get-tuple-element.194), channel_id=1, source_target_pairs={{0,9},{1,8},{2,11},{3,10},{4,13},{5,12},{6,15},{7,14},{8,1},{9,0},... | collective-permute-start | bytes 1996808 | tf_op jit(solution)/shard_map/cond/branch_1_fun/ppermute | solution.py:269
  227.4 4.1 %copy-start.5 = (bf16[25,104,128]{2,1,0:T(8,128)(2,1)S(1)}, bf16[25,104,128]{2,1,0:T(8,128)(2,1)}, u32[]{:S(2)}) copy-start(bf16[25,104,128]{2,1,0:T(8,128)(2,1)} %get-tuple-element.195) | copy-start | bytes 1996804 | tf_op jit(solution)/shard_map/cond
  227.4 4.1 %copy-start.4 = (bf16[25,104,128]{2,1,0:T(8,128)(2,1)S(1)}, bf16[25,104,128]{2,1,0:T(8,128)(2,1)}, u32[]{:S(2)}) copy-start(bf16[25,104,128]{2,1,0:T(8,128)(2,1)} %get-tuple-element.153) | copy-start | bytes 1996804 | tf_op jit(solution)/shard_map/cond
  231.5 20.9 %copy-start.1 = (bf16[25,104,128]{2,1,0:T(8,128)(2,1)}, bf16[25,104,128]{2,1,0:T(8,128)(2,1)S(1)}, u32[]{:S(2)}) copy-start(bf16[25,104,128]{2,1,0:T(8,128)(2,1)S(1)} %collective-permute-done.9.refs_2_) | copy-start | bytes 1996804 | tf_op jit(solution)/shard_map/cond
  231.5 5.9 %collective-permute-start.17 = (bf16[25,104,128]{2,1,0:T(8,128)(2,1)S(1)}, bf16[25,104,128]{2,1,0:T(8,128)(2,1)S(1)}, u32[]{:S(2)}, u32[]{:S(2)}) collective-permute-start(bf16[25,104,128]{2,1,0:T(8,128)(2,1)S(1)} %copy-done.5), channel_id=1, source_target_pairs={{0,1},{1,0},{2,3},{3,2},{4,5},{5,4},{6,7},{7,6},{8,9},{9,8},{10,11... | collective-permute-start | bytes 1996808 | tf_op jit(solution)/shard_map/cond/branch_1_fun/ppermute | solution.py:269
  231.6 19.2 %collective-permute-start.20 = (bf16[25,104,128]{2,1,0:T(8,128)(2,1)S(1)}, bf16[25,104,128]{2,1,0:T(8,128)(2,1)S(1)}, u32[]{:S(2)}, u32[]{:S(2)}) collective-permute-start(bf16[25,104,128]{2,1,0:T(8,128)(2,1)S(1)} %copy-done.4), channel_id=1, source_target_pairs={{0,25},{1,24},{2,27},{3,26},{4,29},{5,28},{6,31},{7,30},{8,17},{9,... | collective-permute-start | bytes 1996808 | tf_op jit(solution)/shard_map/cond/branch_1_fun/ppermute | solution.py:269
  237.3 15.1 %copy-start.2 = (bf16[25,104,128]{2,1,0:T(8,128)(2,1)}, bf16[25,104,128]{2,1,0:T(8,128)(2,1)S(1)}, u32[]{:S(2)}) copy-start(bf16[25,104,128]{2,1,0:T(8,128)(2,1)S(1)} %collective-permute-done.17.refs_4_) | copy-start | bytes 1996804 | tf_op jit(solution)/shard_map/cond
  250.8 1.6 copy-start.3
Sparse Core Ops, SparseCore 0:
  86.3 101.2 all-gather.6
